TPU v7x, 256 devices: a whole 4x4x8 slice. The times are simulated.
256 devices in a mesh: ctx: 32 (over z, x), tp: 8 (over y, core).
Axes of the slice: x: 4, y: 4, z: 8, core: 2. Of those that a mesh axis runs over, the one named last changes fastest.
Arguments:
- tokens: bfloat16 [24576, 4096], P('ctx'), may hold values from -6 to 6
- qkv_weight: bfloat16 [3, 4096, 4096], P(None, 'ctx', 'tp'), may hold values from -0.09375 to 0.09375
- short_filter: float32 [3, 7, 4096], P(None, None, 'tp'), may hold values from -2.4 to 2.4
- long_filter: float32 [256, 128], P('tp'), may hold values from -0.9 to 0.9
- decay_rate: float32 [256], P('tp'), may hold values from 0.004 to 0.2
- skip_gain: float32 [4096], P('tp'), may hold values from -3 to 3
- out_weight: bfloat16 [4096, 4096], P('tp', 'ctx'), may hold values from -0.09375 to 0.09375
Outputs:
- block_out: bfloat16 [24576, 4096], P(('ctx', 'tp'))
All inputs are finite; a program needn't handle non-finite values.
Results may differ from a plain program's by a relative error of at most 0.008.
Values may be sent and summed in bfloat16 or wider, within the bound.
A program may use at most 64 MiB of HBM per device.

v0:
```python
import jax
import jax.numpy as jnp
from jax import lax
from jax.sharding import PartitionSpec as P


def short_conv(extended, short_filter):
    span = short_filter.shape[1]
    length = extended.shape[2] - (span - 1)
    result = short_filter[:, 0, :, None] * extended[:, :, span - 1 :]
    for offset in range(1, span):
        start = span - 1 - offset
        result = result + short_filter[:, offset, :, None] * extended[:, :, start : start + length]
    return result


def banded(filters):
    tap_count = filters.shape[1]
    row_index = jnp.arange(tap_count)[:, None]
    col_index = jnp.arange(tap_count)[None, :]
    distance = (row_index - col_index) % tap_count
    picker = (distance[None, :, :] == jnp.arange(tap_count)[:, None, None]).astype(jnp.bfloat16)
    full_band = jnp.einsum("gk,kij->gij", filters, picker, preferred_element_type=jnp.float32)
    lower_part = row_index >= col_index
    lower_band = jnp.where(lower_part[None], full_band, 0.0).astype(jnp.bfloat16)
    upper_band = jnp.where(lower_part[None], 0.0, full_band).astype(jnp.bfloat16)
    return (lower_band, upper_band)


def long_mix(features, gated, previous, filters, gain):
    channel_count, length = gated.shape
    tap_count = filters.shape[1]
    group_count = filters.shape[0]
    extended = jnp.concatenate([previous, gated], axis=1)
    blocks = extended.reshape(
        group_count, channel_count // group_count, length // tap_count + 1, tap_count
    )
    lower_band, upper_band = banded(filters)
    current = jnp.einsum(
        "gij,gcbj->gcbi", lower_band, blocks[:, :, 1:], preferred_element_type=jnp.float32
    )
    current = current + jnp.einsum(
        "gij,gcbj->gcbi", upper_band, blocks[:, :, :-1], preferred_element_type=jnp.float32
    )
    filtered = current.reshape(channel_count, length)
    return (features[0] * (filtered + gain[:, None] * gated.astype(jnp.float32))).astype(
        jnp.bfloat16
    )


def per_device(tokens, qkv_weight, short_filter, long_filter, decay_rate, skip_gain, out_weight):
    local_width = qkv_weight.shape[2]
    tap_count = long_filter.shape[1]
    span = short_filter.shape[1]
    group_width = local_width // long_filter.shape[0]
    projected = jnp.einsum(
        "tr,src->sct",
        tokens,
        lax.all_gather(qkv_weight, "ctx", axis=1, tiled=True),
        preferred_element_type=jnp.float32,
    )
    qkv = projected.astype(jnp.bfloat16)
    tap_index = jnp.arange(tap_count, dtype=jnp.float32)
    filters = (long_filter * jnp.exp(-decay_rate[:, None] * tap_index[None, :])).astype(
        jnp.bfloat16
    )
    moved = lax.all_to_all(qkv, "ctx", split_axis=1, concat_axis=2, tiled=True)
    share = moved.shape[1]
    position = lax.axis_index("ctx")
    part_short = lax.dynamic_slice_in_dim(short_filter, position * share, share, 2)
    part_filters = lax.dynamic_slice_in_dim(
        filters, position * (share // group_width), share // group_width, 0
    )
    part_gain = lax.dynamic_slice_in_dim(skip_gain, position * share, share, 0)
    leading = jnp.zeros((3, share, span - 1), jnp.bfloat16)
    features = short_conv(jnp.concatenate([leading, moved], axis=2), part_short)
    gated = (features[1] * features[2]).astype(jnp.bfloat16)
    previous = jnp.zeros((share, tap_count), jnp.bfloat16)
    regrouped = long_mix(features, gated, previous, part_filters, part_gain)
    mixed = lax.all_to_all(regrouped, "ctx", split_axis=1, concat_axis=0, tiled=True)
    out_rows = lax.all_gather(out_weight, "ctx", axis=1, tiled=True)
    summed = lax.psum_scatter(
        lax.dot_general(
            mixed, out_rows, (((0,), (0,)), ((), ())), preferred_element_type=jnp.float32
        ),
        "tp",
        scatter_dimension=0,
        tiled=True,
    )
    return summed.astype(jnp.bfloat16)


def solution(mesh):
    in_specs = (
        P("ctx", None),
        P(None, "ctx", "tp"),
        P(None, None, "tp"),
        P("tp", None),
        P("tp"),
        P("tp"),
        P("tp", "ctx"),
    )
    out_specs = P(("ctx", "tp"), None)
    return jax.shard_map(
        per_device, mesh=mesh, in_specs=in_specs, out_specs=out_specs, check_vma=False
    )
```

profile of v0, /device:TPU:1, one launch (start us, length us, event | category | flops | bytes accessed | tf_op | source)
XLA Modules:
  0.0 379.6 jit_solution(5646571431311405019)
XLA Ops:
  6.5 1.9 copy.14
  8.5 127.2 %all-gather.3.cloned.1.call-done = bf16[3,4096,512]{1,2,0:T(8,128)(2,1)} async-done(((bf16[3,128,512]{1,2,0:T(8,128)(2,1)}), bf16[3,4096,512]{1,2,0:T(8,128)(2,1)}) %all-gather.3.cloned.1.call-update) | async-done | bytes 12582928 | tf_op jit(solution)/shard_map/all_gather | solution.py:59
  135.6 14.8 %fusion.4 = bf16[3,512,768]{2,1,0:T(8,128)(2,1)S(1)} fusion(bf16[3,4096,512]{1,2,0:T(8,128)(2,1)} %all-gather.3.cloned.1.call-done, bf16[768,4096]{1,0:T(8,128)(2,1)} %param.7), kind=kOutput, calls=%fused_computation.11 | convolution fusion | flops 9664856064 | bytes 21233664 | tf_op jit(solution)/shard_map/tr,src->sct/dot_general | solution.py:56
  150.4 3.7 copy.15
  154.1 6.8 %all-to-all-start = ((bf16[3,512,768]{2,0,1:T(4,128)(2,1)}), bf16[3,512,768]{2,0,1:T(4,128)(2,1)S(1)}, u32[]{:S(2)}, u32[]{:S(2)}) async-start(bf16[3,512,768]{2,0,1:T(4,128)(2,1)} %copy.15), calls=%async_computation | async-start | bytes 6291456 | tf_op jit(solution)/shard_map/all_to_all | solution.py:67
  161.6 1.1 constant_dynamic-slice_fusion.5
  164.1 1.2 iota_compare_fusion
  165.4 3.5 fusion
  168.8 66.1 %all-to-all-done = bf16[3,512,768]{2,0,1:T(4,128)(2,1)S(1)} async-done(((bf16[3,512,768]{2,0,1:T(4,128)(2,1)}), bf16[3,512,768]{2,0,1:T(4,128)(2,1)S(1)}, u32[]{:S(2)}, u32[]{:S(2)}) %all-to-all-start) | async-done | bytes 2359328 | tf_op jit(solution)/shard_map/all_to_all | solution.py:67
  234.9 3.1 copy.50
  238.0 3.0 all_to_all.28
  241.1 4.9 %multiply_add_fusion = f32[3,16,24576]{2,1,0:T(8,128)S(1)} fusion(bf16[3,16,24576]{2,1,0:T(8,128)(2,1)S(1)} %all_to_all.28, f32[3,16]{1,0:T(4,128)S(1)} %get-tuple-element.14, f32[3,16]{1,0:T(4,128)S(1)} %get-tuple-element.15, f32[3,16]{1,0:T(4,128)S(1)} %get-tuple-element.16, f32[3,16]{1,0:T(4,128)S(1)} %get-tuple-element.17, ...), kind=kLoop, calls=%fused_computation.5 | loop fusion | flops 23592960 | bytes 7079232 | tf_op jit(solution)/shard_map/add | solution.py:13
  246.2 1.0 concatenate.7
  247.1 1.5 reshape.79
  249.0 1.5 convolution_add_fusion
  250.6 2.6 reshape.83
  253.8 0.8 copy-done
  254.7 3.4 fusion.8
  258.0 6.4 %all-to-all-start.1 = ((bf16[16,32,768]{2,0,1:T(8,128)(2,1)}), bf16[16,32,768]{2,0,1:T(8,128)(2,1)S(1)}, u32[]{:S(2)}, u32[]{:S(2)}) async-start(bf16[16,32,768]{2,0,1:T(8,128)(2,1)} %fusion.8), calls=%async_computation.1 | async-start | bytes 1572864 | tf_op jit(solution)/shard_map/all_to_all | solution.py:80
  264.5 7.9 %all-gather.5.cloned.1.call-done = bf16[512,4096]{1,0:T(8,128)(2,1)} async-done(((bf16[512,128]{1,0:T(8,128)(2,1)}), bf16[512,4096]{1,0:T(8,128)(2,1)}) %all-gather.5.cloned.1.call-update) | async-done | bytes 4194320 | tf_op jit(solution)/shard_map/all_gather | solution.py:81
  272.4 15.2 %all-to-all-done.1 = bf16[16,32,768]{2,0,1:T(8,128)(2,1)S(1)} async-done(((bf16[16,32,768]{2,0,1:T(8,128)(2,1)}), bf16[16,32,768]{2,0,1:T(8,128)(2,1)S(1)}, u32[]{:S(2)}, u32[]{:S(2)}) %all-to-all-start.1) | async-done | bytes 786464 | tf_op jit(solution)/shard_map/all_to_all | solution.py:80
  287.6 8.5 %fusion.29 = f32[768,4096]{1,0:T(8,128)} fusion(bf16[512,768]{1,0:T(8,128)(2,1)S(1)} %bitcast.66, bf16[512,4096]{1,0:T(8,128)(2,1)} %all-gather.5.cloned.1.call-done), kind=kOutput, calls=%fused_computation.59 | convolution fusion | flops 3221225472 | bytes 17563648 | tf_op jit(solution)/shard_map/dot_general | solution.py:83
  296.2 74.5 %reduce-scatter.2.cloned.1.call-done = f32[96,4096]{1,0:T(8,128)} async-done(((f32[768,4096]{1,0:T(8,128)}), f32[96,4096]{1,0:T(8,128)}) %reduce-scatter.2.cloned.1.call-update) | async-done | bytes 1572880 | tf_op jit(solution)/shard_map/reduce_scatter | solution.py:82
  370.7 2.4 convert_element_type.74
  (21 shorter events, 3.5 us)
Async XLA Ops:
  6.5 129.1 %all-gather.3.cloned.1.call-start = ((), (), s32[]{:S(2)}) async-start(), calls=%async_computation.3 | async-start | bytes 12976128 | tf_op jit(solution)/shard_map/all_gather | solution.py:59
  154.1 8.6 %copy-start.1 = (f32[32]{0:T(128)S(1)}, f32[32]{0:T(128)}, u32[]{:S(2)}) copy-start(f32[32]{0:T(128)} %param.11) | copy-start | bytes 388
  154.1 80.8 %all-to-all-start = ((bf16[3,512,768]{2,0,1:T(4,128)(2,1)}), bf16[3,512,768]{2,0,1:T(4,128)(2,1)S(1)}, u32[]{:S(2)}, u32[]{:S(2)}) async-start(bf16[3,512,768]{2,0,1:T(4,128)(2,1)} %copy.15), calls=%async_computation | async-start | bytes 6291456 | tf_op jit(solution)/shard_map/all_to_all | solution.py:67
  160.9 111.6 %all-gather.5.cloned.1.call-start = ((), (), s32[]{:S(2)}) async-start(), calls=%async_computation.4 | async-start | bytes 4325376 | tf_op jit(solution)/shard_map/all_gather | solution.py:81
  253.2 1.5 copy-start
  258.0 29.6 %all-to-all-start.1 = ((bf16[16,32,768]{2,0,1:T(8,128)(2,1)}), bf16[16,32,768]{2,0,1:T(8,128)(2,1)S(1)}, u32[]{:S(2)}, u32[]{:S(2)}) async-start(bf16[16,32,768]{2,0,1:T(8,128)(2,1)} %fusion.8), calls=%async_computation.1 | async-start | bytes 1572864 | tf_op jit(solution)/shard_map/all_to_all | solution.py:80
  264.5 106.2 %reduce-scatter.2.cloned.1.call-start = ((), (), s32[]{:S(2)}) async-start(), calls=%async_computation.5 | async-start | bytes 14155776 | tf_op jit(solution)/shard_map/reduce_scatter | solution.py:82
Sparse Core Ops, SparseCore 0:
  9.8 125.8 all-gather.2
  164.1 108.2 all-gather.4
  296.3 74.2 reduce-scatter.1
where the time goes:
time: 380 us
  waiting for transfers between devices  291 us (77%)
  matrix products  28.7 us (8%)
  local copies, waits for them, and re-layouts  20.7 us (5%)
  starting transfers between devices  13.5 us (4%)
  between operations  13.2 us (3%)
  other arithmetic  12.2 us (3%)
    all_gather x1, waiting for transfers between devices, per_device(): lax.all_gather(qkv_weight, 'ctx', axis=1, tiled=True)  127 us
    reduce_scatter x1, waiting for transfers between devices, per_device(): lax.psum_scatter(lax.dot_general(mixed, out_rows, (((0,), (0,)), ((), ())...  74.5 us
    all_to_all x1, waiting for transfers between devices, per_device(): moved = lax.all_to_all(qkv, 'ctx', split_axis=1, concat_axis=2, tiled=True)  66.1 us
    all_to_all x1, waiting for transfers between devices, per_device(): lax.all_to_all(regrouped, 'ctx', split_axis=1, concat_axis=0, tiled=True)  15.2 us
    dot_general x1, matrix products, per_device(): jnp.einsum('tr,src->sct', tokens, lax.all_gather(qkv_weight, 'ctx', axis=...  14.8 us
    dot_general x1, matrix products, per_device(): lax.dot_general(mixed, out_rows, (((0,), (0,)), ((), ())), preferred_elem...  8.55 us
    all_gather x1, waiting for transfers between devices, per_device(): out_rows = lax.all_gather(out_weight, 'ctx', axis=1, tiled=True)  7.9 us
  transfers between devices with their start and end apart: 5, of which 5 were waited for; matrix products, arithmetic and copies ran while one was open for 7% of the time, Pallas kernels for 0%

commit v1 on v0

--- a/solution.py
+++ b/solution.py
@@ -56,7 +56,9 @@
     projected = jnp.einsum(
         "tr,src->sct",
         tokens,
-        lax.all_gather(qkv_weight, "ctx", axis=1, tiled=True),
+        jnp.concatenate(
+            lax.all_to_all(jnp.stack([qkv_weight] * lax.axis_size("ctx")), "ctx", 0, 0), axis=1
+        ),
         preferred_element_type=jnp.float32,
     )
     qkv = projected.astype(jnp.bfloat16)

time: 380 us -> 545 us (1.43)
  blocking collectives: 0 us -> 285 us
  waiting for transfers between devices: 291 us -> 163 us
  local copies, waits for them, and re-layouts: 20.7 us -> 28.4 us
    all_to_all x0 -> x1, blocking collectives: none -> 285 us  [per_device(): lax.all_to_all(jnp.stack([qkv_weight] * lax.axis_size('ctx')), 'ctx', 0, 0)]
    all_gather x1 -> x0, waiting for transfers between devices: 127 us -> none  [per_device(): lax.all_gather(qkv_weight, 'ctx', axis=1, tiled=True)]
    another operation x0 -> x1, local copies, waits for them, and re-layouts: none -> 7.62 us  [per_device(): jnp.stack([qkv_weight] * lax.axis_size('ctx'))]
    all_gather x1, waiting for transfers between devices: 7.9 us -> 1.19 us  [per_device(): out_rows = lax.all_gather(out_weight, 'ctx', axis=1, tiled=True)]
  transfers between devices with their start and end apart: 5 -> 4, of which waited for: 5 -> 4; matrix products, arithmetic and copies ran while one was open for 7% -> 5% of each run, Pallas kernels for 0% -> 0%
where the time goes in v1:
time: 545 us; the launch traced here: 544 us
  blocking collectives  285 us (52%)
  waiting for transfers between devices  163 us (30%)
  local copies, waits for them, and re-layouts  28.4 us (5%)
  matrix products  26.9 us (5%)
  other arithmetic  13.6 us (2%)
  between operations  13.6 us (2%)
  starting transfers between devices  13 us (2%)
    all_to_all x1, blocking collectives, per_device(): lax.all_to_all(jnp.stack([qkv_weight] * lax.axis_size('ctx')), 'ctx', 0, 0)  285 us
    reduce_scatter x1, waiting for transfers between devices, per_device(): lax.psum_scatter(lax.dot_general(mixed, out_rows, (((0,), (0,)), ((), ())...  77.1 us
    all_to_all x1, waiting for transfers between devices, per_device(): moved = lax.all_to_all(qkv, 'ctx', split_axis=1, concat_axis=2, tiled=True)  67.5 us
    all_to_all x1, waiting for transfers between devices, per_device(): lax.all_to_all(regrouped, 'ctx', split_axis=1, concat_axis=0, tiled=True)  17 us
    dot_general x1, matrix products, per_device(): jnp.einsum('tr,src->sct', tokens, jnp.concatenate(lax.all_to_all(jnp.stac...  13 us
  transfers between devices with their start and end apart: 4, of which 4 were waited for; matrix products, arithmetic and copies ran while one was open for 5% of the time, Pallas kernels for 0%

profile of v1, /device:TPU:1, one launch (start us, length us, event | category | flops | bytes accessed | tf_op | source)
XLA Modules:
  0.0 544.0 jit_solution(5288234366000196492)
XLA Ops:
  6.5 1.2 copy.14
  7.8 7.6 %stack.2 = bf16[32,3,128,512]{2,3,1,0:T(8,128)(2,1)} broadcast(bf16[3,128,512]{1,2,0:T(8,128)(2,1)S(1)} %copy.14), dimensions={1,2,3} | broadcast | bytes 12976128 | tf_op jit(solution)/shard_map/stack | solution.py:60
  15.4 285.2 %all_to_all.39 = bf16[32,3,128,512]{2,3,1,0:T(8,128)(2,1)S(1)} all-to-all(bf16[32,3,128,512]{2,3,1,0:T(8,128)(2,1)} %stack.2), channel_id=1, replica_groups=mesh['ctx'=32,'tp'=8] {'ctx'}, dimensions={0} | all-to-all | bytes 25165824 | tf_op jit(solution)/shard_map/all_to_all | solution.py:60
  300.6 13.0 %fusion.6 = bf16[3,512,768]{2,1,0:T(8,128)(2,1)} fusion(bf16[768,4096]{1,0:T(8,128)(2,1)} %param.7, bf16[32,3,128,512]{2,3,1,0:T(8,128)(2,1)S(1)} %all_to_all.39), kind=kOutput, calls=%fused_computation.13 | convolution fusion | flops 9664856064 | bytes 21233664 | tf_op jit(solution)/shard_map/tr,src->sct/dot_general | solution.py:56
  313.6 5.3 copy.16
  318.9 6.5 %all-to-all-start.1 = ((bf16[3,512,768]{2,0,1:T(4,128)(2,1)}), bf16[3,512,768]{2,0,1:T(4,128)(2,1)S(1)}, u32[]{:S(2)}, u32[]{:S(2)}) async-start(bf16[3,512,768]{2,0,1:T(4,128)(2,1)} %copy.16), calls=%async_computation.1 | async-start | bytes 6291456 | tf_op jit(solution)/shard_map/all_to_all | solution.py:69
  326.2 1.1 constant_dynamic-slice_fusion.5
  328.7 1.2 iota_compare_fusion
  330.0 3.5 fusion.3
  333.4 67.5 %all-to-all-done.1 = bf16[3,512,768]{2,0,1:T(4,128)(2,1)S(1)} async-done(((bf16[3,512,768]{2,0,1:T(4,128)(2,1)}), bf16[3,512,768]{2,0,1:T(4,128)(2,1)S(1)}, u32[]{:S(2)}, u32[]{:S(2)}) %all-to-all-start.1) | async-done | bytes 2359328 | tf_op jit(solution)/shard_map/all_to_all | solution.py:69
  400.9 3.1 copy.58
  404.0 3.0 all_to_all.32
  407.0 4.9 multiply_add_fusion
  412.6 1.0 concatenate.7
  413.6 1.5 reshape.89
  415.5 1.5 convolution_add_fusion
  417.0 2.6 reshape.93
  419.8 4.8 fusion.12
  424.6 6.3 %all-to-all-start.2 = ((bf16[16,32,768]{2,0,1:T(8,128)(2,1)}), bf16[16,32,768]{2,0,1:T(8,128)(2,1)S(1)}, u32[]{:S(2)}, u32[]{:S(2)}) async-start(bf16[16,32,768]{2,0,1:T(8,128)(2,1)} %fusion.12), calls=%async_computation.2 | async-start | bytes 1572864 | tf_op jit(solution)/shard_map/all_to_all | solution.py:82
  430.9 1.2 all-gather.2.cloned.1.call-done
  432.1 17.0 %all-to-all-done.2 = bf16[16,32,768]{2,0,1:T(8,128)(2,1)S(1)} async-done(((bf16[16,32,768]{2,0,1:T(8,128)(2,1)}), bf16[16,32,768]{2,0,1:T(8,128)(2,1)S(1)}, u32[]{:S(2)}, u32[]{:S(2)}) %all-to-all-start.2) | async-done | bytes 786464 | tf_op jit(solution)/shard_map/all_to_all | solution.py:82
  449.1 8.5 %fusion.33 = f32[768,4096]{1,0:T(8,128)} fusion(bf16[512,768]{1,0:T(8,128)(2,1)S(1)} %bitcast.75, bf16[512,4096]{1,0:T(8,128)(2,1)} %all-gather.2.cloned.1.call-done), kind=kOutput, calls=%fused_computation.61 | convolution fusion | flops 3221225472 | bytes 17563648 | tf_op jit(solution)/shard_map/dot_general | solution.py:85
  457.6 77.1 %reduce-scatter.2.cloned.1.call-done = f32[96,4096]{1,0:T(8,128)} async-done(((f32[768,4096]{1,0:T(8,128)}), f32[96,4096]{1,0:T(8,128)}) %reduce-scatter.2.cloned.1.call-update) | async-done | bytes 1572880 | tf_op jit(solution)/shard_map/reduce_scatter | solution.py:84
  534.8 2.4 convert_element_type.74
  (18 shorter events, 3.4 us)
Async XLA Ops:
  318.9 8.3 %copy-start = (f32[32]{0:T(128)S(1)}, f32[32]{0:T(128)}, u32[]{:S(2)}) copy-start(f32[32]{0:T(128)} %param.11) | copy-start | bytes 388
  318.9 82.0 %all-to-all-start.1 = ((bf16[3,512,768]{2,0,1:T(4,128)(2,1)}), bf16[3,512,768]{2,0,1:T(4,128)(2,1)S(1)}, u32[]{:S(2)}, u32[]{:S(2)}) async-start(bf16[3,512,768]{2,0,1:T(4,128)(2,1)} %copy.16), calls=%async_computation.1 | async-start | bytes 6291456 | tf_op jit(solution)/shard_map/all_to_all | solution.py:69
  325.4 106.7 %all-gather.2.cloned.1.call-start = ((), (), s32[]{:S(2)}) async-start(), calls=%async_computation.4 | async-start | bytes 4325376 | tf_op jit(solution)/shard_map/all_gather | solution.py:83
  424.6 24.5 %all-to-all-start.2 = ((bf16[16,32,768]{2,0,1:T(8,128)(2,1)}), bf16[16,32,768]{2,0,1:T(8,128)(2,1)S(1)}, u32[]{:S(2)}, u32[]{:S(2)}) async-start(bf16[16,32,768]{2,0,1:T(8,128)(2,1)} %fusion.12), calls=%async_computation.2 | async-start | bytes 1572864 | tf_op jit(solution)/shard_map/all_to_all | solution.py:82
  430.9 103.9 %reduce-scatter.2.cloned.1.call-start = ((), (), s32[]{:S(2)}) async-start(), calls=%async_computation.5 | async-start | bytes 14155776 | tf_op jit(solution)/shard_map/reduce_scatter | solution.py:84
Sparse Core Ops, SparseCore 0:
  328.7 103.3 all-gather.1
  457.8 76.9 reduce-scatter.1
